TPU v7x, 32 devices: a whole 2x2x4 slice. The times are simulated.
32 devices in a mesh: row: 8 (over z, y), col: 4 (over x, core).
Axes of the slice: x: 2, y: 2, z: 4, core: 2. Of those that a mesh axis runs over, the one named last changes fastest.
Arguments:
- upper: bfloat16 [4096, 8, 4, 128], P('row', None, 'col'), as said below
- signs: int32 [4096, 512], P(('row', 'col')), may hold values from 0 to 1
- weights: float32 [4096], P(('row', 'col')), may hold values from 0.5 to 2
- components: float32 [2], replicated, may hold values from 0.3 to 3
Outputs:
- applied: float32 [4096, 512], P(('row', 'col'))
Inputs may be any that keep to these rules, and one draw needn't show every extreme that they name: upper's first dimension and its flattened column index count the same samples in the same order.
All inputs are finite; a program needn't handle non-finite values.
Results may differ from a plain program's by a relative error of at most 0.0055.
Values may be sent and summed in bfloat16 or wider, within the bound.
No kernel may reach another device: no remote copies, remote signals or barrier semaphores. Data moves between devices by JAX's collectives and lax.ppermute only.
A program may use at most 128 MiB of HBM per device.

v0:
```python
import jax
import jax.numpy as jnp
from jax import lax
from jax.sharding import PartitionSpec as P


def body(upper, signs, weights, components):
    rows, ntiles, single, fine = upper.shape
    row_index = lax.axis_index("row")
    col_index = lax.axis_index("col")
    flat = upper.reshape(rows, ntiles * fine)
    probes = ((2 * signs - 1).astype(jnp.float32) * weights[:, None]).astype(jnp.bfloat16)
    q_rows = lax.all_gather(probes, "col", axis=0, tiled=True)
    zero = jnp.zeros((), jnp.bfloat16)
    rowpos = lax.broadcasted_iota(jnp.int32, (rows, ntiles, fine), 0)
    tilepos = lax.broadcasted_iota(jnp.int32, (rows, ntiles, fine), 1)
    colpos = col_index * fine + lax.broadcasted_iota(jnp.int32, (rows, ntiles, fine), 2)
    beyond = tilepos > row_index
    onside = tilepos == row_index
    keep_up = (beyond | onside & (colpos >= rowpos)).reshape(rows, ntiles * fine)
    keep_strict = (beyond | onside & (colpos > rowpos)).reshape(rows, ntiles * fine)
    masked_a = jnp.where(keep_up, flat, zero)
    masked_b = jnp.where(keep_strict, flat, zero)
    columns = masked_a
    direct = jnp.dot(
        columns,
        lax.all_gather(probes, "row", axis=0, tiled=True),
        preferred_element_type=jnp.float32,
    )
    columns = masked_b
    mirrored = lax.psum_scatter(
        lax.dot_general(
            columns, q_rows, (((0,), (0,)), ((), ())), preferred_element_type=jnp.float32
        ).astype(jnp.bfloat16),
        "row",
        scatter_dimension=0,
        tiled=True,
    ).astype(jnp.float32)
    summed = lax.psum_scatter(direct, "col", scatter_dimension=0, tiled=True)
    return components[0] * (summed + mirrored) + components[1] * probes.astype(jnp.float32)


def solution(mesh):
    return jax.shard_map(
        body,
        mesh=mesh,
        in_specs=(P("row", None, "col", None), P(("row", "col"), None), P(("row", "col")), P()),
        out_specs=P(("row", "col"), None),
        check_vma=False,
    )
```

profile of v0, /device:TPU:0, one launch (start us, length us, event | category | flops | bytes accessed | tf_op | source)
XLA Modules:
  0.0 154.1 jit_solution(2603484826157275666)
XLA Ops:
  6.5 0.0 copy-start.3
  6.5 0.0 all-gather.2.cloned.1.call-start
  6.5 1.8 %multiply_convert_fusion = bf16[128,512]{1,0:T(8,128)(2,1)} fusion(s32[128,512]{1,0:T(8,128)} %param.5, f32[128]{0:T(128)} %param.6), kind=kLoop, calls=%fused_computation.23 | loop fusion | flops 327680 | bytes 393728 | tf_op jit(solution)/shard_map/convert_element_type | solution.py:12
  8.3 0.0 all-gather.2.cloned.1.call-update
  8.3 0.0 reduce-scatter.5.cloned.1.call-start
  8.4 8.8 %all_gather.7 = bf16[512,512]{1,0:T(8,128)(2,1)S(1)} all-gather(bf16[128,512]{1,0:T(8,128)(2,1)} %multiply_convert_fusion), channel_id=1, replica_groups=mesh['row'=8,'col'=4] {'col'}, dimensions={0}, use_global_device_ids=true | all-gather | bytes 655360 | tf_op jit(solution)/shard_map/all_gather | solution.py:13
  17.3 0.1 broadcast_bitcast_fusion.1
  17.3 0.1 broadcast_bitcast_fusion.2
  17.4 0.0 copy-done.3
  17.4 1.8 %convolution_convert_fusion = bf16[1024,512]{1,0:T(8,128)(2,1)} fusion(bf16[512,512]{1,0:T(8,128)(2,1)S(1)} %all_gather.7, s32[1024]{0:T(1024)S(1)} %broadcast_bitcast_fusion, pred[1024]{0:T(1024)(128)(4,1)S(1)} %broadcast_bitcast_fusion.1, pred[1024]{0:T(1024)(128)(4,1)S(1)} %broadcast_bitcast_fusion.2, bf16[64,8,8,128]{3,2,1,0:T(8,128)(2,1)S(1)} %bitcast.22), kind=kOutput, calls=%fused_computation.8 | convolution fusion | flops 539492352 | bytes 2627584 | tf_op jit(solution)/shard_map/dot_general | solution.py:32
  19.2 0.0 reduce-scatter.5.cloned.1.call-update
  19.2 0.0 reduce-scatter.3.cloned.1.call-start
  19.3 33.1 %all-gather.2.cloned.1.call-done = bf16[1024,512]{1,0:T(8,128)(2,1)} async-done(((bf16[128,512]{1,0:T(8,128)(2,1)}), bf16[1024,512]{1,0:T(8,128)(2,1)}) %all-gather.2.cloned.1.call-update) | async-done | bytes 1048592 | tf_op jit(solution)/shard_map/all_gather | solution.py:27
  52.4 3.0 %fusion.7 = f32[512,512]{1,0:T(8,128)} fusion(bf16[1024,512]{1,0:T(8,128)(2,1)} %all-gather.2.cloned.1.call-done, s32[1024]{0:T(1024)S(1)} %broadcast_bitcast_fusion, pred[1024]{0:T(1024)(128)(4,1)S(1)} %broadcast_bitcast_fusion.1, pred[1024]{0:T(1024)(128)(4,1)S(1)} %broadcast_bitcast_fusion.2, bf16[64,8,8,128]{3,2,1,0:T(8,128)(2,1)S(1)} %bitcast.23), kind=kOutput, calls=%fused_computation.9 | convolution fusion | flops 538968064 | bytes 3151872 | tf_op jit(solution)/shard_map/dot_general | solution.py:25
  55.3 0.0 copy-start.2
  55.3 0.0 copy-start
  55.3 0.0 copy-start.1
  55.3 0.0 reduce-scatter.3.cloned.1.call-update
  55.4 0.6 copy-done.2
  56.0 0.6 fusion.23
  56.6 61.3 %reduce-scatter.5.cloned.1.call-done = bf16[128,512]{1,0:T(8,128)(2,1)} async-done(((bf16[1024,512]{1,0:T(8,128)(2,1)}), bf16[128,512]{1,0:T(8,128)(2,1)}) %reduce-scatter.5.cloned.1.call-update) | async-done | bytes 131088 | tf_op jit(solution)/shard_map/reduce_scatter | solution.py:31
  117.9 26.6 %reduce-scatter.3.cloned.1.call-done = f32[128,512]{1,0:T(8,128)} async-done(((f32[512,512]{1,0:T(8,128)}), f32[128,512]{1,0:T(8,128)}) %reduce-scatter.3.cloned.1.call-update) | async-done | bytes 262160 | tf_op jit(solution)/shard_map/reduce_scatter | solution.py:39
  144.5 0.0 copy-done
  144.5 0.0 copy-done.1
  144.5 3.1 %multiply_add_fusion = f32[128,512]{1,0:T(8,128)} fusion(f32[128,512]{1,0:T(8,128)} %reduce-scatter.3.cloned.1.call-done, bf16[128,512]{1,0:T(8,128)(2,1)} %reduce-scatter.5.cloned.1.call-done, f32[]{:T(128)} %bitcast.4, f32[]{:T(128)} %bitcast, f32[128]{0:T(128)S(1)} %copy-done.1, s32[128,512]{1,0:T(8,128)S(1)} %copy-done), kind=kLoop, calls=%fused_computation.22 | loop fusion | flops 720896 | bytes 918024 | tf_op jit(solution)/shard_map/add | solution.py:40
  (3 shorter events, 0.0 us)
Async XLA Ops:
  6.5 10.9 %copy-start.3 = (bf16[512,8,1,128]{3,1,2,0:T(8,128)(2,1)S(1)}, bf16[512,8,1,128]{3,1,2,0:T(8,128)(2,1)}, u32[]{:S(2)}) copy-start(bf16[512,8,1,128]{3,1,2,0:T(8,128)(2,1)} %param.4) | copy-start | bytes 3145732
  6.5 45.8 %all-gather.2.cloned.1.call-start = ((), (), s32[]{:S(2)}) async-start(), calls=%async_computation.2 | async-start | bytes 1179648 | tf_op jit(solution)/shard_map/all_gather | solution.py:27
  8.3 109.5 %reduce-scatter.5.cloned.1.call-start = ((), (), s32[]{:S(2)}) async-start(), calls=%async_computation.4 | async-start | bytes 1179648 | tf_op jit(solution)/shard_map/reduce_scatter | solution.py:31
  19.2 125.3 %reduce-scatter.3.cloned.1.call-start = ((), (), s32[]{:S(2)}) async-start(), calls=%async_computation.3 | async-start | bytes 1310720 | tf_op jit(solution)/shard_map/reduce_scatter | solution.py:39
  55.3 0.7 copy-start.2
  55.3 89.2 %copy-start = (s32[128,512]{1,0:T(8,128)S(1)}, s32[128,512]{1,0:T(8,128)}, u32[]{:S(2)}) copy-start(s32[128,512]{1,0:T(8,128)} %param.5) | copy-start | bytes 786436
  55.3 89.2 %copy-start.1 = (f32[128]{0:T(128)S(1)}, f32[128]{0:T(128)}, u32[]{:S(2)}) copy-start(f32[128]{0:T(128)} %param.6) | copy-start | bytes 1540
Sparse Core Ops, SparseCore 0:
  9.5 42.8 all-gather.1
  55.8 62.0 reduce-scatter.4
  120.6 23.8 reduce-scatter.2
where the time goes:
time: 154 us
  waiting for transfers between devices  121 us (79%)
  between operations  13.1 us (9%)
  blocking collectives  8.83 us (6%)
  other arithmetic  4.85 us (3%)
  matrix products  4.75 us (3%)
    reduce_scatter x1, waiting for transfers between devices, body(): lax.psum_scatter(lax.dot_general(columns, q_rows, (((0,), (0,)), ((), ())...  61.3 us
    all_gather x1, waiting for transfers between devices, body(): lax.all_gather(probes, 'row', axis=0, tiled=True)  33.1 us
    reduce_scatter x1, waiting for transfers between devices, body(): summed = lax.psum_scatter(direct, 'col', scatter_dimension=0, tiled=True)  26.6 us
    all_gather x1, blocking collectives, body(): q_rows = lax.all_gather(probes, 'col', axis=0, tiled=True)  8.83 us
  transfers between devices with their start and end apart: 3, of which 3 were waited for; matrix products, arithmetic and copies ran while one was open for 4% of the time, Pallas kernels for 0%

commit v1 on v0

--- a/solution.py
+++ b/solution.py
@@ -2,6 +2,23 @@
 import jax.numpy as jnp
 from jax import lax
 from jax.sharding import PartitionSpec as P
+
+
+def joined_along(blocks, dim):
+    blocks = jnp.moveaxis(blocks, 0, dim)
+    shape = blocks.shape
+    return blocks.reshape(*shape[:dim], shape[dim] * shape[dim + 1], *shape[dim + 2 :])
+
+
+def gather_around(x, axis, dim):
+    peers = lax.axis_size(axis)
+    upward = [(i, (i + 1) % peers) for i in range(peers)]
+    parts = [x]
+    while len(parts) < peers:
+        parts.append(lax.ppermute(parts[-1], axis, upward))
+    index = lax.axis_index(axis)
+    parts = jnp.stack(parts)[(index - jnp.arange(peers)) % peers]
+    return joined_along(parts, dim)
 
 
 def body(upper, signs, weights, components):
@@ -22,11 +39,7 @@
     masked_a = jnp.where(keep_up, flat, zero)
     masked_b = jnp.where(keep_strict, flat, zero)
     columns = masked_a
-    direct = jnp.dot(
-        columns,
-        lax.all_gather(probes, "row", axis=0, tiled=True),
-        preferred_element_type=jnp.float32,
-    )
+    direct = jnp.dot(columns, gather_around(probes, "row", 0), preferred_element_type=jnp.float32)
     columns = masked_b
     mirrored = lax.psum_scatter(
         lax.dot_general(

time: 154 us -> 123 us (0.80)
  waiting for transfers between devices: 121 us -> 86.8 us
  starting transfers between devices: 0.09 us -> 4.65 us
  blocking collectives: 8.83 us -> 7.16 us
    reduce_scatter x1, waiting for transfers between devices: 61.3 us -> 12.1 us  [body(): lax.psum_scatter(lax.dot_general(columns, q_rows, (((0,), (0,)), ((), ())...]
    ppermute x0 -> x7, waiting for transfers between devices: none -> 48 us  [gather_around(): parts.append(lax.ppermute(parts[-1], axis, upward))]
    all_gather x1 -> x0, waiting for transfers between devices: 33.1 us -> none  [body(): lax.all_gather(probes, 'row', axis=0, tiled=True)]
    ppermute x0 -> x7, starting transfers between devices: none -> 4.6 us  [gather_around(): parts.append(lax.ppermute(parts[-1], axis, upward))]
    convert_element_type x1 -> x0, other arithmetic: 1.78 us -> none  [body(): ((2 * signs - 1).astype(jnp.float32) * weights[:, None]).astype(jnp.bfloa...]
    all_gather x1, blocking collectives: 8.83 us -> 7.16 us  [body(): q_rows = lax.all_gather(probes, 'col', axis=0, tiled=True)]
  transfers between devices with their start and end apart: 3 -> 9, of which waited for: 3 -> 8; matrix products, arithmetic and copies ran while one was open for 4% -> 5% of each run, Pallas kernels for 0% -> 0%
where the time goes in v1:
time: 123 us; the launch traced here: 122 us
  waiting for transfers between devices  86.8 us (71%)
  between operations  13.5 us (11%)
  blocking collectives  7.16 us (6%)
  other arithmetic  4.82 us (4%)
  starting transfers between devices  4.65 us (4%)
  matrix products  3.51 us (3%)
  local copies, waits for them, and re-layouts  2.11 us (2%)
    ppermute x7, waiting for transfers between devices, gather_around(): parts.append(lax.ppermute(parts[-1], axis, upward))  48 us
    reduce_scatter x1, waiting for transfers between devices, body(): summed = lax.psum_scatter(direct, 'col', scatter_dimension=0, tiled=True)  26.6 us
    reduce_scatter x1, waiting for transfers between devices, body(): lax.psum_scatter(lax.dot_general(columns, q_rows, (((0,), (0,)), ((), ())...  12.1 us
    all_gather x1, blocking collectives, body(): q_rows = lax.all_gather(probes, 'col', axis=0, tiled=True)  7.16 us
    ppermute x7, starting transfers between devices, gather_around(): parts.append(lax.ppermute(parts[-1], axis, upward))  4.6 us
    add x1, other arithmetic, body(): components[0] * (summed + mirrored)  3.06 us
  transfers between devices with their start and end apart: 9, of which 8 were waited for; matrix products, arithmetic and copies ran while one was open for 5% of the time, Pallas kernels for 0%

profile of v1, /device:TPU:0, one launch (start us, length us, event | category | flops | bytes accessed | tf_op | source)
XLA Modules:
  0.0 122.5 jit_solution(8605430916927143803)
XLA Ops:
  6.5 0.0 reduce-scatter.5.cloned.1.call-start
  6.5 1.1 bitcast_dynamic-update-slice_fusion.7
  7.7 3.0 %collective-permute-start = (bf16[128,512]{1,0:T(8,128)(2,1)S(1)}, bf16[128,512]{1,0:T(8,128)(2,1)S(1)}, u32[]{:S(2)}, u32[]{:S(2)}) collective-permute-start(bf16[128,512]{1,0:T(8,128)(2,1)S(1)} %get-tuple-element.6), channel_id=1, source_target_pairs={{0,4},{4,8},{8,12},{12,16},{16,20},{20,24},{24,28},{28,0},{1,5},{5... | collective-permute-start | bytes 393224 | tf_op jit(solution)/shard_map/ppermute | solution.py:18
  10.7 7.2 %all_gather.3 = bf16[512,512]{1,0:T(8,128)(2,1)S(1)} all-gather(bf16[128,512]{1,0:T(8,128)(2,1)S(1)} %get-tuple-element.6), channel_id=1, replica_groups=mesh['row'=8,'col'=4] {'col'}, dimensions={0}, use_global_device_ids=true | all-gather | bytes 655360 | tf_op jit(solution)/shard_map/all_gather | solution.py:30
  17.9 0.1 broadcast_bitcast_fusion.1
  17.9 0.1 broadcast_bitcast_fusion.2
  18.0 0.0 copy-done
  18.0 1.8 %convolution_convert_fusion = bf16[1024,512]{1,0:T(8,128)(2,1)} fusion(bf16[512,512]{1,0:T(8,128)(2,1)S(1)} %all_gather.3, bf16[64,8,8,128]{3,2,1,0:T(8,128)(2,1)S(1)} %bitcast.44, s32[1024]{0:T(1024)S(1)} %broadcast_bitcast_fusion, pred[1024]{0:T(1024)(128)(4,1)S(1)} %broadcast_bitcast_fusion.1, pred[1024]{0:T(1024)(128)(4,1)S(1)} %broadcast_bitcast_fusion.2), kind=kOutput, calls=%fused_computation.9 | convolution fusion | flops 539492352 | bytes 2627584 | tf_op jit(solution)/shard_map/dot_general | solution.py:45
  19.8 0.0 reduce-scatter.5.cloned.1.call-update
  19.8 0.0 reduce-scatter.3.cloned.1.call-start
  19.9 0.6 fusion.2
  20.5 0.0 collective-permute-done
  20.5 1.6 %collective-permute-start.1 = (bf16[128,512]{1,0:T(8,128)(2,1)S(1)}, bf16[128,512]{1,0:T(8,128)(2,1)S(1)}, u32[]{:S(2)}, u32[]{:S(2)}) collective-permute-start(bf16[128,512]{1,0:T(8,128)(2,1)S(1)} %collective-permute-done), channel_id=1, source_target_pairs={{0,4},{4,8},{8,12},{12,16},{16,20},{20,24},{24,28},{28,0},{1,5},{5... | collective-permute-start | bytes 393224 | tf_op jit(solution)/shard_map/ppermute | solution.py:18
  22.1 6.9 %collective-permute-done.1 = bf16[128,512]{1,0:T(8,128)(2,1)S(1)} collective-permute-done((bf16[128,512]{1,0:T(8,128)(2,1)S(1)}, bf16[128,512]{1,0:T(8,128)(2,1)S(1)}, u32[]{:S(2)}, u32[]{:S(2)}) %collective-permute-start.1) | collective-permute-done | bytes 131104 | tf_op jit(solution)/shard_map/ppermute | solution.py:18
  29.1 0.0 collective-permute-start.2
  29.1 9.2 %collective-permute-done.2 = bf16[128,512]{1,0:T(8,128)(2,1)S(1)} collective-permute-done((bf16[128,512]{1,0:T(8,128)(2,1)S(1)}, bf16[128,512]{1,0:T(8,128)(2,1)S(1)}, u32[]{:S(2)}, u32[]{:S(2)}) %collective-permute-start.2) | collective-permute-done | bytes 131104 | tf_op jit(solution)/shard_map/ppermute | solution.py:18
  38.3 0.0 collective-permute-start.3
  38.3 8.6 %collective-permute-done.3 = bf16[128,512]{1,0:T(8,128)(2,1)S(1)} collective-permute-done((bf16[128,512]{1,0:T(8,128)(2,1)S(1)}, bf16[128,512]{1,0:T(8,128)(2,1)S(1)}, u32[]{:S(2)}, u32[]{:S(2)}) %collective-permute-start.3) | collective-permute-done | bytes 131104 | tf_op jit(solution)/shard_map/ppermute | solution.py:18
  46.9 0.0 collective-permute-start.4
  47.0 7.8 %collective-permute-done.4 = bf16[128,512]{1,0:T(8,128)(2,1)S(1)} collective-permute-done((bf16[128,512]{1,0:T(8,128)(2,1)S(1)}, bf16[128,512]{1,0:T(8,128)(2,1)S(1)}, u32[]{:S(2)}, u32[]{:S(2)}) %collective-permute-start.4) | collective-permute-done | bytes 131104 | tf_op jit(solution)/shard_map/ppermute | solution.py:18
  54.7 0.0 collective-permute-start.5
  54.7 7.8 %collective-permute-done.5 = bf16[128,512]{1,0:T(8,128)(2,1)S(1)} collective-permute-done((bf16[128,512]{1,0:T(8,128)(2,1)S(1)}, bf16[128,512]{1,0:T(8,128)(2,1)S(1)}, u32[]{:S(2)}, u32[]{:S(2)}) %collective-permute-start.5) | collective-permute-done | bytes 131104 | tf_op jit(solution)/shard_map/ppermute | solution.py:18
  62.5 0.0 collective-permute-start.6
  62.5 7.6 %collective-permute-done.6 = bf16[128,512]{1,0:T(8,128)(2,1)S(1)} collective-permute-done((bf16[128,512]{1,0:T(8,128)(2,1)S(1)}, bf16[128,512]{1,0:T(8,128)(2,1)S(1)}, u32[]{:S(2)}, u32[]{:S(2)}) %collective-permute-start.6) | collective-permute-done | bytes 131104 | tf_op jit(solution)/shard_map/ppermute | solution.py:18
  70.2 0.6 gather_fusion
  70.8 1.7 %fusion.9 = f32[512,512]{1,0:T(8,128)} fusion(bf16[1024,512]{1,0:T(8,128)(2,1)S(1)} %bitcast.43, bf16[64,8,8,128]{3,2,1,0:T(8,128)(2,1)S(1)} %bitcast.45), kind=kOutput, calls=%fused_computation.12 | convolution fusion | flops 536870912 | bytes 3145728 | tf_op jit(solution)/shard_map/dot_general | solution.py:42
  72.5 0.0 reduce-scatter.3.cloned.1.call-update
  72.5 0.6 copy-done.1
  73.2 0.6 fusion.19
  73.8 12.1 %reduce-scatter.5.cloned.1.call-done = bf16[128,512]{1,0:T(8,128)(2,1)} async-done(((bf16[1024,512]{1,0:T(8,128)(2,1)}), bf16[128,512]{1,0:T(8,128)(2,1)}) %reduce-scatter.5.cloned.1.call-update) | async-done | bytes 131088 | tf_op jit(solution)/shard_map/reduce_scatter | solution.py:44
  85.9 26.6 %reduce-scatter.3.cloned.1.call-done = f32[128,512]{1,0:T(8,128)} async-done(((f32[512,512]{1,0:T(8,128)}), f32[128,512]{1,0:T(8,128)}) %reduce-scatter.3.cloned.1.call-update) | async-done | bytes 262160 | tf_op jit(solution)/shard_map/reduce_scatter | solution.py:52
  112.6 3.1 %multiply_add_fusion = f32[128,512]{1,0:T(8,128)} fusion(bf16[128,512]{1,0:T(8,128)(2,1)S(1)} %get-tuple-element.6, f32[128,512]{1,0:T(8,128)} %reduce-scatter.3.cloned.1.call-done, bf16[128,512]{1,0:T(8,128)(2,1)} %reduce-scatter.5.cloned.1.call-done, f32[]{:T(128)} %bitcast.14, f32[]{:T(128)} %bitcast), kind=kLoop, calls=%fused_computation.19 | loop fusion | flops 393216 | bytes 786440 | tf_op jit(solution)/shard_map/add | solution.py:53
  (14 shorter events, 0.1 us)
Async XLA Ops:
  6.5 11.5 %copy-start = (bf16[512,8,1,128]{3,1,2,0:T(8,128)(2,1)S(1)}, bf16[512,8,1,128]{3,1,2,0:T(8,128)(2,1)}, u32[]{:S(2)}) copy-start(bf16[512,8,1,128]{3,1,2,0:T(8,128)(2,1)} %param.4) | copy-start | bytes 3145732
  6.5 79.4 %reduce-scatter.5.cloned.1.call-start = ((), (), s32[]{:S(2)}) async-start(), calls=%async_computation.3 | async-start | bytes 1179648 | tf_op jit(solution)/shard_map/reduce_scatter | solution.py:44
  7.7 12.8 %collective-permute-start = (bf16[128,512]{1,0:T(8,128)(2,1)S(1)}, bf16[128,512]{1,0:T(8,128)(2,1)S(1)}, u32[]{:S(2)}, u32[]{:S(2)}) collective-permute-start(bf16[128,512]{1,0:T(8,128)(2,1)S(1)} %get-tuple-element.6), channel_id=1, source_target_pairs={{0,4},{4,8},{8,12},{12,16},{16,20},{20,24},{24,28},{28,0},{1,5},{5... | collective-permute-start | bytes 393224 | tf_op jit(solution)/shard_map/ppermute | solution.py:18
  19.8 92.7 %reduce-scatter.3.cloned.1.call-start = ((), (), s32[]{:S(2)}) async-start(), calls=%async_computation.2 | async-start | bytes 1310720 | tf_op jit(solution)/shard_map/reduce_scatter | solution.py:52
  20.5 8.5 %collective-permute-start.1 = (bf16[128,512]{1,0:T(8,128)(2,1)S(1)}, bf16[128,512]{1,0:T(8,128)(2,1)S(1)}, u32[]{:S(2)}, u32[]{:S(2)}) collective-permute-start(bf16[128,512]{1,0:T(8,128)(2,1)S(1)} %collective-permute-done), channel_id=1, source_target_pairs={{0,4},{4,8},{8,12},{12,16},{16,20},{20,24},{24,28},{28,0},{1,5},{5... | collective-permute-start | bytes 393224 | tf_op jit(solution)/shard_map/ppermute | solution.py:18
  29.1 9.3 %collective-permute-start.2 = (bf16[128,512]{1,0:T(8,128)(2,1)S(1)}, bf16[128,512]{1,0:T(8,128)(2,1)S(1)}, u32[]{:S(2)}, u32[]{:S(2)}) collective-permute-start(bf16[128,512]{1,0:T(8,128)(2,1)S(1)} %collective-permute-done.1), channel_id=1, source_target_pairs={{0,4},{4,8},{8,12},{12,16},{16,20},{20,24},{24,28},{28,0},{1,5},{5... | collective-permute-start | bytes 393224 | tf_op jit(solution)/shard_map/ppermute | solution.py:18
  38.3 8.6 %collective-permute-start.3 = (bf16[128,512]{1,0:T(8,128)(2,1)S(1)}, bf16[128,512]{1,0:T(8,128)(2,1)S(1)}, u32[]{:S(2)}, u32[]{:S(2)}) collective-permute-start(bf16[128,512]{1,0:T(8,128)(2,1)S(1)} %collective-permute-done.2), channel_id=1, source_target_pairs={{0,4},{4,8},{8,12},{12,16},{16,20},{20,24},{24,28},{28,0},{1,5},{5... | collective-permute-start | bytes 393224 | tf_op jit(solution)/shard_map/ppermute | solution.py:18
  46.9 7.8 %collective-permute-start.4 = (bf16[128,512]{1,0:T(8,128)(2,1)S(1)}, bf16[128,512]{1,0:T(8,128)(2,1)S(1)}, u32[]{:S(2)}, u32[]{:S(2)}) collective-permute-start(bf16[128,512]{1,0:T(8,128)(2,1)S(1)} %collective-permute-done.3), channel_id=1, source_target_pairs={{0,4},{4,8},{8,12},{12,16},{16,20},{20,24},{24,28},{28,0},{1,5},{5... | collective-permute-start | bytes 393224 | tf_op jit(solution)/shard_map/ppermute | solution.py:18
  54.7 7.8 %collective-permute-start.5 = (bf16[128,512]{1,0:T(8,128)(2,1)S(1)}, bf16[128,512]{1,0:T(8,128)(2,1)S(1)}, u32[]{:S(2)}, u32[]{:S(2)}) collective-permute-start(bf16[128,512]{1,0:T(8,128)(2,1)S(1)} %collective-permute-done.4), channel_id=1, source_target_pairs={{0,4},{4,8},{8,12},{12,16},{16,20},{20,24},{24,28},{28,0},{1,5},{5... | collective-permute-start | bytes 393224 | tf_op jit(solution)/shard_map/ppermute | solution.py:18
  62.5 7.7 %collective-permute-start.6 = (bf16[128,512]{1,0:T(8,128)(2,1)S(1)}, bf16[128,512]{1,0:T(8,128)(2,1)S(1)}, u32[]{:S(2)}, u32[]{:S(2)}) collective-permute-start(bf16[128,512]{1,0:T(8,128)(2,1)S(1)} %collective-permute-done.5), channel_id=1, source_target_pairs={{0,4},{4,8},{8,12},{12,16},{16,20},{20,24},{24,28},{28,0},{1,5},{5... | collective-permute-start | bytes 393224 | tf_op jit(solution)/shard_map/ppermute | solution.py:18
  72.5 0.7 copy-start.1
Sparse Core Ops, SparseCore 0:
  20.0 65.9 reduce-scatter.4
  88.6 23.9 reduce-scatter.2
